TPU v7x, 32 devices: a whole 2x2x4 slice. The times are simulated.
32 devices in a mesh: tissue: 2 (over x), sample: 4 (over y, core), variant: 4 (over z).
Axes of the slice: x: 2, y: 2, z: 4, core: 2. Of those that a mesh axis runs over, the one named last changes fastest.
Arguments:
- dosage: bfloat16 [52, 512, 512], P('tissue', 'sample', 'variant'), may hold values from 0 to 2
- express: bfloat16 [52, 512, 2048], P('tissue', 'sample', 'variant'), may hold values from -6 to 6
- covar: float32 [52, 32, 512], P('tissue', None, 'sample'), may hold values from -6 to 6
- member: int32 [52, 512], P('tissue', 'sample'), may hold values 0 or 1
- live: int32 [52], replicated, may hold values 0 or 1
- mixing: float32 [52, 52], replicated, may hold values from -1 to 2, as said below
Outputs:
- chi_stat: float32 [512, 2048], P('variant', 'sample')
- meta_stat: float32 [512, 2048], P('variant', 'sample')
Inputs may be any that keep to these rules, and one draw needn't show every extreme that they name: mixing is the identity plus a dense spread of off-diagonal and diagonal terms.
All inputs are finite; a program needn't handle non-finite values. No bound on the sum of `member` on one device may be relied on, other than what follows from the above.
Results may differ from a plain program's by a relative error of at most 0.019.
Values may be sent and summed in bfloat16 or wider, within the bound.
A program may use at most 128 MiB of HBM per device.

v0:
```python
import jax
import jax.numpy as jnp
from jax import lax
from jax.sharding import PartitionSpec as P


def solve_small(factor_low, rhs_matrix):
    forward = lax.linalg.triangular_solve(factor_low, rhs_matrix, left_side=True, lower=True)
    return lax.linalg.triangular_solve(
        factor_low, forward, left_side=True, lower=True, transpose_a=True
    )


def body(dosage, express, covar, member, live, mixing):
    highest = lax.Precision.HIGHEST
    tis_dev = dosage.shape[0]
    n_cov = covar.shape[1]
    weights = member.astype(jnp.float32)
    dos_masked = dosage.astype(jnp.float32) * weights[:, :, None]
    cov_masked = covar * weights[:, None, :]
    gram_part = jnp.einsum("tks,tjs->tkj", cov_masked, cov_masked, precision=highest)
    amat_part = jnp.einsum("tks,tsv->tkv", cov_masked, dos_masked, precision=highest)
    count_part = jnp.sum(weights, axis=1)
    gsq_part = jnp.sum(dos_masked * dos_masked, axis=1)
    identity = jnp.eye(n_cov, dtype=jnp.float32)
    gathered = lax.all_gather(express, "variant", axis=2, tiled=True)
    exp_masked = gathered.astype(jnp.float32) * weights[:, :, None]
    bmat_part = jnp.einsum("tks,tsg->tkg", cov_masked, exp_masked, precision=highest)
    esq_part = jnp.sum(exp_masked * exp_masked, axis=1)
    gram_sum, amat_sum, counts, gsq_sum, bmat_sum, esq_sum = (
        lax.psum(gram_part.astype(jnp.bfloat16), "sample").astype(jnp.float32),
        lax.psum(amat_part.astype(jnp.bfloat16), "sample").astype(jnp.float32),
        lax.psum(count_part.astype(jnp.bfloat16), "sample").astype(jnp.float32),
        lax.psum(gsq_part.astype(jnp.bfloat16), "sample").astype(jnp.float32),
        lax.psum(bmat_part.astype(jnp.bfloat16), "sample").astype(jnp.float32),
        lax.psum(esq_part.astype(jnp.bfloat16), "sample").astype(jnp.float32),
    )
    factor_low = jnp.linalg.cholesky(gram_sum + identity)
    proj_exp = solve_small(factor_low, bmat_sum)
    eres = (
        exp_masked - jnp.einsum("tks,tkg->tsg", cov_masked, proj_exp, precision=highest)
    ).astype(jnp.bfloat16)
    enorm = esq_sum - jnp.sum(bmat_sum * proj_exp, axis=1)
    proj_dos = solve_small(factor_low, amat_sum)
    gres = (
        dos_masked - jnp.einsum("tks,tkv->tsv", cov_masked, proj_dos, precision=highest)
    ).astype(jnp.bfloat16)
    gnorm = gsq_sum - jnp.sum(amat_sum * proj_dos, axis=1)
    n_genes = eres.shape[2]
    gene_share = n_genes // lax.axis_size("sample")
    cross = lax.psum_scatter(
        jnp.einsum("tse,tsv->etv", eres, gres, preferred_element_type=jnp.float32).astype(
            jnp.bfloat16
        ),
        "sample",
        scatter_dimension=0,
        tiled=True,
    ).astype(jnp.float32)
    gene_start = lax.axis_index("sample") * gene_share
    enorm_slice = lax.dynamic_slice_in_dim(enorm, gene_start, gene_share, 1)
    tissue_start = lax.axis_index("tissue") * tis_dev
    live_f = live.astype(jnp.float32)
    live_own = lax.dynamic_slice_in_dim(live_f, tissue_start, tis_dev, 0)
    scales = live_own * jnp.sqrt(jnp.maximum(counts - n_cov, 1.0))
    inv_var = 1.0 / jnp.sqrt(gnorm + 1e-05)
    inv_gene = 1.0 / jnp.sqrt(enorm_slice + 1e-05)
    zvals = (
        cross * scales[None, :, None] * inv_var[None, :, :] * jnp.transpose(inv_gene)[:, :, None]
    )
    own_rows = lax.dynamic_slice_in_dim(mixing, tissue_start, tis_dev, 0)
    mixed = jnp.zeros_like(zvals) + jnp.einsum(
        "ut,gtv->guv",
        own_rows,
        lax.all_gather(zvals.astype(jnp.bfloat16), "tissue", axis=1, tiled=True).astype(
            jnp.float32
        ),
        precision=highest,
    )
    mixed = mixed * live_own[None, :, None]
    nlive = jnp.maximum(jnp.sum(live_f), 1.0)
    chi_part = jnp.sum(mixed * mixed, axis=1) / nlive
    meta_part = jnp.sum(mixed, axis=1) / jnp.sqrt(nlive)
    chi_stat, meta_stat = (
        lax.psum(chi_part.astype(jnp.bfloat16), "tissue").astype(jnp.float32),
        lax.psum(meta_part.astype(jnp.bfloat16), "tissue").astype(jnp.float32),
    )
    return (jnp.transpose(chi_stat), jnp.transpose(meta_stat))


def solution(mesh):
    return jax.shard_map(
        body,
        mesh=mesh,
        in_specs=(
            P("tissue", "sample", "variant"),
            P("tissue", "sample", "variant"),
            P("tissue", None, "sample"),
            P("tissue", "sample"),
            P(),
            P(),
        ),
        out_specs=(P("variant", "sample"), P("variant", "sample")),
        check_vma=False,
    )
```

profile of v0, /device:TPU:0, one launch (start us, length us, event | category | flops | bytes accessed | tf_op | source)
XLA Modules:
  0.0 751.9 jit_solution(18436027038904383437)
XLA Ops:
  8.7 3.7 fusion.8
  12.4 235.3 %all-gather.3.cloned.1.call-done = bf16[26,128,2048]{2,1,0:T(8,128)(2,1)} async-done(((bf16[26,128,512]{2,1,0:T(8,128)(2,1)}), bf16[26,128,2048]{2,1,0:T(8,128)(2,1)}) %all-gather.3.cloned.1.call-update) | async-done | bytes 13631504 | tf_op jit(solution)/shard_map/all_gather | solution.py:26
  247.6 19.7 %fusion.6 = bf16[26,32,2048]{2,1,0:T(8,128)(2,1)} fusion(bf16[26,128,2048]{2,1,0:T(8,128)(2,1)} %all-gather.3.cloned.1.call-done, f32[26,128]{1,0:T(8,128)S(1)} %convert_element_type.83, f32[26,32,128]{2,1,0:T(8,128)} %param.8), kind=kOutput, calls=%fused_computation.14 | convolution fusion | flops 2632687616 | bytes 17478656 | tf_op jit(solution)/shard_map/tks,tsg->tkg/dot_general | solution.py:28
  267.4 10.8 %multiply_reduce_fusion = bf16[26,2048]{1,0:T(8,128)(2,1)} fusion(bf16[26,128,2048]{2,1,0:T(8,128)(2,1)} %all-gather.3.cloned.1.call-done, f32[26,128]{1,0:T(8,128)S(1)} %convert_element_type.83), kind=kLoop, calls=%fused_computation | loop fusion | flops 27209728 | bytes 13751296 | tf_op jit(solution)/shard_map/reduce_sum | solution.py:29
  278.2 10.6 %reduce-scatter.2.cloned.1.call-start = ((), (), s32[]{:S(2)}) async-start(), calls=%async_computation.2 | async-start | bytes 17039360 | tf_op jit(solution)/shard_map/reduce_scatter | solution.py:51
  289.5 0.8 convolution_convert_fusion.1
  290.3 19.6 %all-reduce = (bf16[26,32,32]{1,2,0:T(8,128)(2,1)S(1)}, bf16[26,128]{1,0:T(8,128)(2,1)S(1)}, bf16[26]{0:T(256)(128)(2,1)S(1)}) all-reduce(bf16[26,32,32]{1,2,0:T(8,128)(2,1)S(1)} %convolution_convert_fusion.1, bf16[26,128]{1,0:T(8,128)(2,1)S(1)} %multiply_reduce_fusion.2, ...), channel_id=1, replica_groups=mesh['tissue'=2,'sample'=4,'variant'=4] {'sample'}, use_global_device_ids=true, to_apply=%region_0.0 | all-reduce | flops 29978 | bytes 119912 | tf_op jit(solution)/shard_map/psum | solution.py:31
  310.2 76.2 %custom-call.13 = f32[26,32,32]{2,1,0:T(8,128)S(1)} custom-call(f32[26,32,32]{2,1,0:T(8,128)S(1)} %fusion.18), custom_call_target="Cholesky" | custom-call | tf_op jit(solution)/shard_map/jit(cholesky)/cholesky | solution.py:38
  386.7 64.7 %custom-call.14 = f32[26,1,32,32]{2,3,1,0:T(8,128)} custom-call(f32[26,1,32,32]{3,2,1,0:T(8,128)S(1)} %select_bitcast_fusion), custom_call_target="InvertDiagBlocksLowerTriangular" | custom-call | tf_op jit(solution)/shard_map/triangular_solve | solution.py:9
  451.5 5.2 fusion.12
  456.8 8.4 %multiply_reduce_fusion.1 = (f32[26,2048]{1,0:T(8,128)}, f32[26,32,2048]{2,1,0:T(8,128)S(1)}) fusion(bf16[26,32,2048]{2,1,0:T(8,128)(2,1)S(1)} %copy-done.3, f32[26,32,2048]{2,1,0:T(8,128)S(1)} %fusion.12, f32[26,1,32,32]{2,3,1,0:T(8,128)S(1)} %copy-done.6), kind=kOutput, calls=%fused_computation.13 | convolution fusion | flops 659369984 | bytes 17358848 | tf_op jit(solution)/shard_map/triangular_solve | solution.py:9
  466.3 3.4 subtract_convert_fusion.1
  469.7 27.1 %subtract_convert_fusion = bf16[26,128,2048]{2,1,0:T(8,128)(2,1)} fusion(bf16[26,128,2048]{2,1,0:T(8,128)(2,1)S(1)} %bitcast.46, f32[26,32,2048]{2,1,0:T(8,128)S(1)} %get-tuple-element.19, f32[26,128]{1,0:T(8,128)S(1)} %convert_element_type.83, f32[26,32,128]{2,1,0:T(8,128)} %param.8), kind=kOutput, calls=%fused_computation.1 | convolution fusion | flops 2644615168 | bytes 34518016 | tf_op jit(solution)/shard_map/tks,tkg->tsg/dot_general | solution.py:41
  496.8 13.5 %fusion.2 = bf16[2048,26,128]{0,2,1:T(8,128)(2,1)} fusion(bf16[26,128,128]{2,1,0:T(8,128)(2,1)S(1)} %subtract_convert_fusion.1, bf16[26,128,2048]{2,1,0:T(8,128)(2,1)} %subtract_convert_fusion), kind=kOutput, calls=%fused_computation.6 | convolution fusion | flops 1751646208 | bytes 28114944 | tf_op jit(solution)/shard_map/tse,tsv->etv/dot_general | solution.py:52
  511.1 0.9 fusion.33
  511.9 99.5 %reduce-scatter.2.cloned.1.call-done = bf16[512,26,128]{0,2,1:T(8,128)(2,1)} async-done(((bf16[2048,26,128]{0,2,1:T(8,128)(2,1)}), bf16[512,26,128]{0,2,1:T(8,128)(2,1)}) %reduce-scatter.2.cloned.1.call-update) | async-done | bytes 3407888 | tf_op jit(solution)/shard_map/reduce_scatter | solution.py:51
  611.4 2.8 multiply_convert_fusion
  614.2 3.6 copy.23
  619.2 85.1 %all-gather.5.cloned.1.call-done = bf16[512,52,128]{2,0,1:T(8,128)(2,1)} async-done(((bf16[512,26,128]{2,0,1:T(8,128)(2,1)}), bf16[512,52,128]{2,0,1:T(8,128)(2,1)}) %all-gather.5.cloned.1.call-update) | async-done | bytes 6815760 | tf_op jit(solution)/shard_map/all_gather | solution.py:74
  704.3 12.9 %bitcast_reduce_fusion = (f32[512,128]{1,0:T(8,128)S(1)}, f32[512,128]{1,0:T(8,128)S(1)}) fusion(f32[26]{0:T(128)S(1)} %get-tuple-element.17, f32[52,52]{1,0:T(8,128)S(1)} %copy-done, s32[]{:T(128)S(6)} %select_n.12, bf16[512,52,128]{2,0,1:T(8,128)(2,1)} %all-gather.5.cloned.1.call-done), kind=kOutput, calls=%fused_computation.7 | convolution fusion | flops 1069940736 | bytes 7356932 | tf_op jit(solution)/shard_map/ut,gtv->guv/dot_general | solution.py:71
  717.2 0.8 fusion.29
  718.0 23.5 %all-reduce.8.cloned.1.call-done = (bf16[128,512]{0,1:T(8,128)(2,1)}, bf16[128,512]{0,1:T(8,128)(2,1)}) async-done(((bf16[128,512]{0,1:T(8,128)(2,1)}, bf16[128,512]{0,1:T(8,128)(2,1)}), (bf16[128,512]{0,1:T(8,128)(2,1)}, bf16[128,512]{0,1:T(8,128)(2,1)})) %all-reduce.8.cloned.1.call-update) | async-done | bytes 262160 | tf_op jit(solution)/shard_map/psum | solution.py:84
  741.5 1.7 copy.25
  743.2 1.7 copy.26
  (58 shorter events, 5.4 us)
Async XLA Ops:
  7.2 697.1 %copy-start = (f32[52,52]{1,0:T(8,128)S(1)}, f32[52,52]{1,0:T(8,128)}, u32[]{:S(2)}) copy-start(f32[52,52]{1,0:T(8,128)} %param.11) | copy-start | bytes 32452
  7.2 240.5 %all-gather.3.cloned.1.call-start = ((), (), s32[]{:S(2)}) async-start(), calls=%async_computation.1 | async-start | bytes 17039360 | tf_op jit(solution)/shard_map/all_gather | solution.py:26
  7.9 443.5 %all-reduce.6.cloned.1.call-start = ((), (), s32[]{:S(2)}) async-start(), calls=%async_computation.4 | async-start | bytes 7503872 | tf_op jit(solution)/shard_map/psum | solution.py:32
  267.4 21.5 %copy-start.8 = (s32[26,128]{1,0:T(8,128)S(1)}, s32[26,128]{1,0:T(8,128)}, u32[]{:S(2)}) copy-start(s32[26,128]{1,0:T(8,128)} %param.9) | copy-start | bytes 39940
  267.4 21.6 %copy-start.4 = (bf16[26,128,128]{2,1,0:T(8,128)(2,1)S(1)}, bf16[26,128,128]{2,1,0:T(8,128)(2,1)}, u32[]{:S(2)}) copy-start(bf16[26,128,128]{2,1,0:T(8,128)(2,1)} %param.6) | copy-start | bytes 2555908
  267.4 22.1 %copy-start.1 = (f32[26,32,128]{2,1,0:T(8,128)S(1)}, f32[26,32,128]{2,1,0:T(8,128)}, u32[]{:S(2)}) copy-start(f32[26,32,128]{2,1,0:T(8,128)} %param.8) | copy-start | bytes 1277956
  278.2 333.2 %reduce-scatter.2.cloned.1.call-start = ((), (), s32[]{:S(2)}) async-start(), calls=%async_computation.2 | async-start | bytes 17039360 | tf_op jit(solution)/shard_map/reduce_scatter | solution.py:51
  451.4 5.2 copy-start.3
  451.4 5.3 copy-start.6
  451.5 18.2 %slice-start = ((s8[13631488]{0:T(1024)(128)(4,1)}), s8[4194304]{0:T(1024)(128)(4,1)S(1)}, s32[]{:S(2)}) async-start(s8[13631488]{0:T(1024)(128)(4,1)} %bitcast.45), calls=%async_computation.6 | async-start | bytes 8388608
  451.5 18.2 %slice-start.1 = ((s8[13631488]{0:T(1024)(128)(4,1)}), s8[4194304]{0:T(1024)(128)(4,1)S(1)}, s32[]{:S(2)}) async-start(s8[13631488]{0:T(1024)(128)(4,1)} %bitcast.45), calls=%async_computation.7 | async-start | bytes 8388608
  456.7 8.4 %copy-start.7 = (bf16[26,32,128]{2,1,0:T(8,128)(2,1)S(1)}, bf16[26,32,128]{2,1,0:T(8,128)(2,1)}, u32[]{:S(2)}) copy-start(bf16[26,32,128]{2,1,0:T(8,128)(2,1)} %get-tuple-element.11) | copy-start | bytes 638980
  456.7 9.5 %copy-start.2 = (f32[26,32,128]{2,1,0:T(8,128)S(1)}, f32[26,32,128]{2,1,0:T(8,128)}, u32[]{:S(2)}) copy-start(f32[26,32,128]{2,1,0:T(8,128)} %param.8) | copy-start | bytes 1277956
  456.7 9.5 %copy-start.5 = (bf16[26,128,128]{2,1,0:T(8,128)(2,1)S(1)}, bf16[26,128,128]{2,1,0:T(8,128)(2,1)}, u32[]{:S(2)}) copy-start(bf16[26,128,128]{2,1,0:T(8,128)(2,1)} %param.6) | copy-start | bytes 2555908
  456.7 13.0 %slice-start.2 = ((s8[13631488]{0:T(1024)(128)(4,1)}), s8[4194304]{0:T(1024)(128)(4,1)S(1)}, s32[]{:S(2)}) async-start(s8[13631488]{0:T(1024)(128)(4,1)} %bitcast.45), calls=%async_computation.8 | async-start | bytes 8388608
  456.8 13.0 %slice-start.3 = ((s8[13631488]{0:T(1024)(128)(4,1)}), s8[1048576]{0:T(1024)(128)(4,1)S(1)}, s32[]{:S(2)}) async-start(s8[13631488]{0:T(1024)(128)(4,1)} %bitcast.45), calls=%async_computation.9 | async-start | bytes 2097152
  510.3 0.7 copy-start.9
  510.4 193.9 %all-gather.5.cloned.1.call-start = ((), (), s32[]{:S(2)}) async-start(), calls=%async_computation.3 | async-start | bytes 10223616 | tf_op jit(solution)/shard_map/all_gather | solution.py:74
  617.9 123.6 %all-reduce.8.cloned.1.call-start = ((), (), s32[]{:S(2)}) async-start(), calls=%async_computation.5 | async-start | bytes 524288 | tf_op jit(solution)/shard_map/psum | solution.py:84
Sparse Core Ops, SparseCore 0:
  9.6 238.0 all-gather.2
  278.3 80.5 all-reduce.5
  510.5 100.8 reduce-scatter.1
  618.0 86.2 all-gather.4
  718.1 23.3 all-reduce.7
where the time goes:
time: 760 us; the launch traced here: 752 us
  waiting for transfers between devices  444 us (58%)
  other arithmetic  159 us (21%)
  matrix products  95.8 us (13%)
  blocking collectives  19.6 us (3%)
  between operations  15.2 us (2%)
  starting transfers between devices  10.7 us (1%)
  local copies, waits for them, and re-layouts  7.88 us (1%)
    all_gather x1, waiting for transfers between devices, body(): gathered = lax.all_gather(express, 'variant', axis=2, tiled=True)  235 us
    reduce_scatter x1, waiting for transfers between devices, body(): lax.psum_scatter(jnp.einsum('tse,tsv->etv', eres, gres, preferred_element...  99.5 us
    all_gather x1, waiting for transfers between devices, body(): lax.all_gather(zvals.astype(jnp.bfloat16), 'tissue', axis=1, tiled=True)  85.1 us
    another operation x4, other arithmetic, body(): factor_low = jnp.linalg.cholesky(gram_sum + identity)  76.4 us
    another operation x3, other arithmetic, solve_small(): lax.linalg.triangular_solve(factor_low, forward, left_side=True, lower=Tr...  64.9 us
    dot_general x1, matrix products, body(): jnp.einsum('tks,tkg->tsg', cov_masked, proj_exp, precision=highest)  27.1 us
    psum x1, waiting for transfers between devices, body(): lax.psum(chi_part.astype(jnp.bfloat16), 'tissue').astype(jnp.float32)  23.5 us
    dot_general x1, matrix products, body(): jnp.einsum('tks,tsg->tkg', cov_masked, exp_masked, precision=highest)  19.7 us
  transfers between devices with their start and end apart: 5, of which 4 were waited for; matrix products, arithmetic and copies ran while one was open for 20% of the time, Pallas kernels for 0%

commit v1 on v0

--- a/solution.py
+++ b/solution.py
@@ -2,6 +2,17 @@
 import jax.numpy as jnp
 from jax import lax
 from jax.sharding import PartitionSpec as P
+
+
+def gather_around(shard, axis, dim):
+    ways = lax.axis_size(axis)
+    pieces = [shard]
+    for far in range(1, ways):
+        pieces.append(
+            lax.ppermute(pieces[far - 1], axis, [(d, (d - 1) % ways) for d in range(ways)])
+        )
+    line = jnp.concatenate(pieces, axis=dim)
+    return jnp.roll(line, lax.axis_index(axis) * shard.shape[dim], axis=dim)
 
 
 def solve_small(factor_low, rhs_matrix):
@@ -23,7 +34,7 @@
     count_part = jnp.sum(weights, axis=1)
     gsq_part = jnp.sum(dos_masked * dos_masked, axis=1)
     identity = jnp.eye(n_cov, dtype=jnp.float32)
-    gathered = lax.all_gather(express, "variant", axis=2, tiled=True)
+    gathered = gather_around(express, "variant", 2)
     exp_masked = gathered.astype(jnp.float32) * weights[:, :, None]
     bmat_part = jnp.einsum("tks,tsg->tkg", cov_masked, exp_masked, precision=highest)
     esq_part = jnp.sum(exp_masked * exp_masked, axis=1)

time: 760 us -> 763 us (level)
  local copies, waits for them, and re-layouts: 7.88 us -> 30.4 us
  waiting for transfers between devices: 444 us -> 422 us
    all_gather x1 -> x0, waiting for transfers between devices: 235 us -> none  [body(): gathered = lax.all_gather(express, 'variant', axis=2, tiled=True)]
    ppermute x0 -> x3, waiting for transfers between devices: none -> 208 us  [gather_around(): lax.ppermute(pieces[far - 1], axis, [(d, (d - 1) % ways) for d in range(w...]
    unnamed x30 -> x31, local copies, waits for them, and re-layouts: 4.06 us -> 24.2 us
    ppermute x0 -> x3, starting transfers between devices: none -> 13.7 us  [gather_around(): lax.ppermute(pieces[far - 1], axis, [(d, (d - 1) % ways) for d in range(w...]
    reduce_scatter x1, starting transfers between devices: 10.6 us -> 0.04 us  [body(): lax.psum_scatter(jnp.einsum('tse,tsv->etv', eres, gres, preferred_element...]
  transfers between devices with their start and end apart: 5 -> 7, of which waited for: 4 -> 6; matrix products, arithmetic and copies ran while one was open for 20% -> 20% of each run, Pallas kernels for 0% -> 0%
where the time goes in v1:
time: 763 us; the launch traced here: 759 us
  waiting for transfers between devices  422 us (55%)
  other arithmetic  159 us (21%)
  matrix products  103 us (13%)
  local copies, waits for them, and re-layouts  30.4 us (4%)
  blocking collectives  15.8 us (2%)
  between operations  15 us (2%)
  starting transfers between devices  13.9 us (2%)
    ppermute x3, waiting for transfers between devices, gather_around(): lax.ppermute(pieces[far - 1], axis, [(d, (d - 1) % ways) for d in range(w...  208 us
    reduce_scatter x1, waiting for transfers between devices, body(): lax.psum_scatter(jnp.einsum('tse,tsv->etv', eres, gres, preferred_element...  105 us
    all_gather x1, waiting for transfers between devices, body(): lax.all_gather(zvals.astype(jnp.bfloat16), 'tissue', axis=1, tiled=True)  85.1 us
    another operation x4, other arithmetic, body(): factor_low = jnp.linalg.cholesky(gram_sum + identity)  76.4 us
    another operation x3, other arithmetic, solve_small(): lax.linalg.triangular_solve(factor_low, forward, left_side=True, lower=Tr...  64.8 us
    dot_general x1, matrix products, body(): jnp.einsum('tks,tkg->tsg', cov_masked, proj_exp, precision=highest)  28.2 us
    unnamed x31, local copies, waits for them, and re-layouts  24.2 us
    psum x1, waiting for transfers between devices, body(): lax.psum(chi_part.astype(jnp.bfloat16), 'tissue').astype(jnp.float32)  23.5 us
  transfers between devices with their start and end apart: 7, of which 6 were waited for; matrix products, arithmetic and copies ran while one was open for 20% of the time, Pallas kernels for 0%

profile of v1, /device:TPU:0, one launch (start us, length us, event | category | flops | bytes accessed | tf_op | source)
XLA Modules:
  0.0 759.2 jit_solution(11523505248698018070)
XLA Ops:
  7.2 5.1 collective-permute-start
  12.4 73.3 %collective-permute-done = bf16[26,128,512]{2,1,0:T(8,128)(2,1)S(1)} collective-permute-done((bf16[26,128,512]{2,1,0:T(8,128)(2,1)}, bf16[26,128,512]{2,1,0:T(8,128)(2,1)S(1)}, u32[]{:S(2)}, u32[]{:S(2)}) %collective-permute-start) | collective-permute-done | bytes 3407904 | tf_op jit(solution)/shard_map/ppermute | solution.py:12
  85.6 4.2 collective-permute-start.1
  89.8 72.1 %collective-permute-done.1 = bf16[26,128,512]{2,1,0:T(8,128)(2,1)} collective-permute-done((bf16[26,128,512]{2,1,0:T(8,128)(2,1)S(1)}, bf16[26,128,512]{2,1,0:T(8,128)(2,1)}, u32[]{:S(2)}, u32[]{:S(2)}) %collective-permute-start.1) | collective-permute-done | bytes 3407904 | tf_op jit(solution)/shard_map/ppermute | solution.py:12
  161.9 4.4 collective-permute-start.2
  172.4 2.5 constant_dynamic-update-slice_fusion.5
  175.0 62.9 %collective-permute-done.2 = bf16[26,128,512]{2,1,0:T(8,128)(2,1)} collective-permute-done((bf16[26,128,512]{2,1,0:T(8,128)(2,1)}, bf16[26,128,512]{2,1,0:T(8,128)(2,1)}, u32[]{:S(2)}, u32[]{:S(2)}) %collective-permute-start.2) | collective-permute-done | bytes 3407904 | tf_op jit(solution)/shard_map/ppermute | solution.py:12
  246.1 9.0 %copy-done.1 = bf16[26,128,4096]{2,1,0:T(8,128)(2,1)} copy-done((bf16[26,128,4096]{2,1,0:T(8,128)(2,1)}, bf16[26,128,4096]{2,1,0:T(8,128)(2,1)S(1)}, u32[]{:S(2)}) %copy-start.1) | copy-done | bytes 27263000
  255.1 18.0 %fusion.7 = bf16[26,32,2048]{2,1,0:T(8,128)(2,1)} fusion(f32[26,128]{1,0:T(8,128)S(1)} %convert_element_type.83, bf16[26,128,4096]{2,1,0:T(8,128)(2,1)S(1)} %constant_dynamic-update-slice_fusion, s32[]{:T(128)S(6)} %select_n.26, f32[26,32,128]{2,1,0:T(8,128)S(1)} %copy-done.4), kind=kOutput, calls=%fused_computation.15 | convolution fusion | flops 2632687616 | bytes 17498116 | tf_op jit(solution)/shard_map/tks,tsg->tkg/dot_general | solution.py:39
  273.1 10.8 %multiply_reduce_fusion = bf16[26,2048]{1,0:T(8,128)(2,1)} fusion(f32[26,128]{1,0:T(8,128)S(1)} %convert_element_type.83, bf16[26,128,4096]{2,1,0:T(8,128)(2,1)} %copy-done.1, s32[]{:T(128)S(6)} %select_n.26), kind=kLoop, calls=%fused_computation | loop fusion | flops 27209728 | bytes 13751300 | tf_op jit(solution)/shard_map/reduce_sum | solution.py:40
  285.5 15.8 %all-reduce = (bf16[26,32,32]{1,2,0:T(8,128)(2,1)S(1)}, bf16[26,128]{1,0:T(8,128)(2,1)S(1)}, bf16[26]{0:T(256)(128)(2,1)S(1)}) all-reduce(bf16[26,32,32]{1,2,0:T(8,128)(2,1)S(1)} %convolution_convert_fusion.1, bf16[26,128]{1,0:T(8,128)(2,1)S(1)} %multiply_reduce_fusion.2, ...), channel_id=1, replica_groups=mesh['tissue'=2,'sample'=4,'variant'=4] {'sample'}, use_global_device_ids=true, to_apply=%region_0.0 | all-reduce | flops 29978 | bytes 119912 | tf_op jit(solution)/shard_map/psum | solution.py:42
  301.7 76.2 %custom-call.13 = f32[26,32,32]{2,1,0:T(8,128)S(1)} custom-call(f32[26,32,32]{2,1,0:T(8,128)S(1)} %fusion.19), custom_call_target="Cholesky" | custom-call | tf_op jit(solution)/shard_map/jit(cholesky)/cholesky | solution.py:49
  378.2 64.7 %custom-call.14 = f32[26,1,32,32]{2,3,1,0:T(8,128)} custom-call(f32[26,1,32,32]{3,2,1,0:T(8,128)S(1)} %select_bitcast_fusion), custom_call_target="InvertDiagBlocksLowerTriangular" | custom-call | tf_op jit(solution)/shard_map/triangular_solve | solution.py:20
  442.9 6.7 fusion.13
  449.6 12.6 %multiply_reduce_fusion.1 = (f32[26,2048]{1,0:T(8,128)}, f32[26,32,2048]{2,1,0:T(8,128)}) fusion(bf16[26,32,2048]{2,1,0:T(8,128)(2,1)} %get-tuple-element.12, f32[26,32,2048]{2,1,0:T(8,128)} %fusion.13, f32[26,1,32,32]{2,3,1,0:T(8,128)S(1)} %copy-done.8), kind=kOutput, calls=%fused_computation.14 | convolution fusion | flops 659369984 | bytes 17358848 | tf_op jit(solution)/shard_map/triangular_solve | solution.py:20
  462.2 28.2 %subtract_convert_fusion = bf16[26,128,2048]{2,1,0:T(8,128)(2,1)} fusion(f32[26,32,2048]{2,1,0:T(8,128)} %get-tuple-element.19, f32[26,128]{1,0:T(8,128)S(1)} %convert_element_type.83, bf16[26,128,4096]{2,1,0:T(8,128)(2,1)S(1)} %copy-done.2, s32[]{:T(128)S(6)} %select_n.26, f32[26,32,128]{2,1,0:T(8,128)} %param.8), kind=kOutput, calls=%fused_computation.1 | convolution fusion | flops 2644615168 | bytes 34537476 | tf_op jit(solution)/shard_map/tks,tkg->tsg/dot_general | solution.py:52
  493.7 4.5 subtract_convert_fusion.1
  498.1 13.5 %fusion.2 = bf16[2048,26,128]{0,2,1:T(8,128)(2,1)} fusion(bf16[26,128,128]{2,1,0:T(8,128)(2,1)S(1)} %subtract_convert_fusion.1, bf16[26,128,2048]{2,1,0:T(8,128)(2,1)} %subtract_convert_fusion), kind=kOutput, calls=%fused_computation.6 | convolution fusion | flops 1751646208 | bytes 28114944 | tf_op jit(solution)/shard_map/tse,tsv->etv/dot_general | solution.py:63
  513.3 105.4 %reduce-scatter.2.cloned.1.call-done = bf16[512,26,128]{0,2,1:T(8,128)(2,1)} async-done(((bf16[2048,26,128]{0,2,1:T(8,128)(2,1)}), bf16[512,26,128]{0,2,1:T(8,128)(2,1)}) %reduce-scatter.2.cloned.1.call-update) | async-done | bytes 3407888 | tf_op jit(solution)/shard_map/reduce_scatter | solution.py:62
  618.6 2.8 multiply_convert_fusion
  621.5 3.6 copy.23
  626.4 85.1 %all-gather.2.cloned.1.call-done = bf16[512,52,128]{2,0,1:T(8,128)(2,1)} async-done(((bf16[512,26,128]{2,0,1:T(8,128)(2,1)}), bf16[512,52,128]{2,0,1:T(8,128)(2,1)}) %all-gather.2.cloned.1.call-update) | async-done | bytes 6815760 | tf_op jit(solution)/shard_map/all_gather | solution.py:85
  711.5 13.1 %bitcast_reduce_fusion = (f32[512,128]{1,0:T(8,128)S(1)}, f32[512,128]{1,0:T(8,128)S(1)}) fusion(f32[26]{0:T(128)S(1)} %get-tuple-element.17, f32[52,52]{1,0:T(8,128)S(1)} %copy-done, s32[]{:T(128)S(6)} %select_n.27, bf16[512,52,128]{2,0,1:T(8,128)(2,1)} %all-gather.2.cloned.1.call-done), kind=kOutput, calls=%fused_computation.8 | convolution fusion | flops 1069940736 | bytes 7356932 | tf_op jit(solution)/shard_map/ut,gtv->guv/dot_general | solution.py:82
  725.5 23.5 %all-reduce.8.cloned.1.call-done = (bf16[128,512]{0,1:T(8,128)(2,1)}, bf16[128,512]{0,1:T(8,128)(2,1)}) async-done(((bf16[128,512]{0,1:T(8,128)(2,1)}, bf16[128,512]{0,1:T(8,128)(2,1)}), (bf16[128,512]{0,1:T(8,128)(2,1)}, bf16[128,512]{0,1:T(8,128)(2,1)})) %all-reduce.8.cloned.1.call-update) | async-done | bytes 262160 | tf_op jit(solution)/shard_map/psum | solution.py:95
  (62 shorter events, 26.1 us)
Async XLA Ops:
  7.2 704.4 %copy-start = (f32[52,52]{1,0:T(8,128)S(1)}, f32[52,52]{1,0:T(8,128)}, u32[]{:S(2)}) copy-start(f32[52,52]{1,0:T(8,128)} %param.11) | copy-start | bytes 32452
  7.2 435.7 %all-reduce.6.cloned.1.call-start = ((), (), s32[]{:S(2)}) async-start(), calls=%async_computation.3 | async-start | bytes 7503872 | tf_op jit(solution)/shard_map/psum | solution.py:43
  7.2 78.4 %collective-permute-start = (bf16[26,128,512]{2,1,0:T(8,128)(2,1)}, bf16[26,128,512]{2,1,0:T(8,128)(2,1)S(1)}, u32[]{:S(2)}, u32[]{:S(2)}) collective-permute-start(bf16[26,128,512]{2,1,0:T(8,128)(2,1)} %param.7), channel_id=1, source_target_pairs={{0,3},{1,0},{2,1},{3,2},{4,7},{5,4},{6,5},{7,6},{8,11},{9,8},{10,9... | collective-permute-start | bytes 10223624 | tf_op jit(solution)/shard_map/ppermute | solution.py:12
  85.6 76.3 %collective-permute-start.1 = (bf16[26,128,512]{2,1,0:T(8,128)(2,1)S(1)}, bf16[26,128,512]{2,1,0:T(8,128)(2,1)}, u32[]{:S(2)}, u32[]{:S(2)}) collective-permute-start(bf16[26,128,512]{2,1,0:T(8,128)(2,1)S(1)} %collective-permute-done), channel_id=1, source_target_pairs={{0,3},{1,0},{2,1},{3,2},{4,7},{5,4},{6,5},{7,6},{8,11},{9,8},{10,9... | collective-permute-start | bytes 10223624 | tf_op jit(solution)/shard_map/ppermute | solution.py:12
  161.9 76.0 %collective-permute-start.2 = (bf16[26,128,512]{2,1,0:T(8,128)(2,1)}, bf16[26,128,512]{2,1,0:T(8,128)(2,1)}, u32[]{:S(2)}, u32[]{:S(2)}) collective-permute-start(bf16[26,128,512]{2,1,0:T(8,128)(2,1)} %collective-permute-done.1), channel_id=1, source_target_pairs={{0,3},{1,0},{2,1},{3,2},{4,7},{5,4},{6,5},{7,6},{8,11},{9,8},{10,9... | collective-permute-start | bytes 10223624 | tf_op jit(solution)/shard_map/ppermute | solution.py:12
  167.0 2.5 copy-start.4
  167.1 2.5 copy-start.6
  172.4 67.9 %copy-start.3 = (bf16[26,128,512]{2,1,0:T(8,128)(2,1)S(1)}, bf16[26,128,512]{2,1,0:T(8,128)(2,1)}, u32[]{:S(2)}) copy-start(bf16[26,128,512]{2,1,0:T(8,128)(2,1)} %param.7) | copy-start | bytes 10223620
  246.1 9.0 %copy-start.1 = (bf16[26,128,4096]{2,1,0:T(8,128)(2,1)}, bf16[26,128,4096]{2,1,0:T(8,128)(2,1)S(1)}, u32[]{:S(2)}) copy-start(bf16[26,128,4096]{2,1,0:T(8,128)(2,1)S(1)} %constant_dynamic-update-slice_fusion) | copy-start | bytes 81788928
  273.1 11.0 %copy-start.9 = (s32[26,128]{1,0:T(8,128)S(1)}, s32[26,128]{1,0:T(8,128)}, u32[]{:S(2)}) copy-start(s32[26,128]{1,0:T(8,128)} %param.9) | copy-start | bytes 39940
  273.1 11.1 %copy-start.7 = (bf16[26,128,128]{2,1,0:T(8,128)(2,1)S(1)}, bf16[26,128,128]{2,1,0:T(8,128)(2,1)}, u32[]{:S(2)}) copy-start(bf16[26,128,128]{2,1,0:T(8,128)(2,1)} %param.6) | copy-start | bytes 2555908
  273.1 11.6 %copy-start.5 = (f32[26,32,128]{2,1,0:T(8,128)S(1)}, f32[26,32,128]{2,1,0:T(8,128)}, u32[]{:S(2)}) copy-start(f32[26,32,128]{2,1,0:T(8,128)} %param.8) | copy-start | bytes 1277956
  283.9 334.7 %reduce-scatter.2.cloned.1.call-start = ((), (), s32[]{:S(2)}) async-start(), calls=%async_computation.1 | async-start | bytes 17039360 | tf_op jit(solution)/shard_map/reduce_scatter | solution.py:62
  442.9 6.7 copy-start.8
  442.9 19.3 %copy-start.2 = (bf16[26,128,4096]{2,1,0:T(8,128)(2,1)S(1)}, bf16[26,128,4096]{2,1,0:T(8,128)(2,1)}, u32[]{:S(2)}) copy-start(bf16[26,128,4096]{2,1,0:T(8,128)(2,1)} %copy-done.1) | copy-start | bytes 81788928
  511.7 0.7 copy-start.10
  511.7 199.8 %all-gather.2.cloned.1.call-start = ((), (), s32[]{:S(2)}) async-start(), calls=%async_computation.2 | async-start | bytes 10223616 | tf_op jit(solution)/shard_map/all_gather | solution.py:85
  625.1 123.9 %all-reduce.8.cloned.1.call-start = ((), (), s32[]{:S(2)}) async-start(), calls=%async_computation.4 | async-start | bytes 524288 | tf_op jit(solution)/shard_map/psum | solution.py:95
Sparse Core Ops, SparseCore 0:
  284.1 82.8 all-reduce.5
  511.8 106.7 reduce-scatter.1
  625.2 86.2 all-gather.1
  725.6 23.3 all-reduce.7
